TPU v7x, 512 devices: a whole 4x8x8 slice. The times are simulated.
512 devices in a mesh: dp: 128 (over y, z, core), grp: 4 (over x).
Axes of the slice: x: 4, y: 8, z: 8, core: 2. Of those that a mesh axis runs over, the one named last changes fastest.
Arguments:
- states: bfloat16 [65536, 2048], P(('dp', 'grp')), may hold values from -60 to 60
- projection: bfloat16 [2048, 768], replicated, may hold values from -0.125 to 0.125
- owner_group: int32 [65536, 1], P(('dp', 'grp')), may hold values from 0 to 127; in each aligned block of 128 rows (0 to 127, 128 to 255, ...) at most 2 rows name the same one
- cluster_sub: int32 [65536], P(('dp', 'grp')), may hold values from 0 to 3
- priority: int32 [65536], P(('dp', 'grp')), may hold values from 0 to 65535, each once
Outputs:
- dup_score: float32 [65536], P(('dp', 'grp'))
Inputs may be any that keep to these rules, and one draw needn't show every extreme that they name: `owner_group`: in each aligned block of 128 rows (the rows of one device) no owner is named by more than 2 rows; in some block some owner is named by exactly 2 rows.
All inputs are finite; a program needn't handle non-finite values.
Results may differ from a plain program's by a relative error of at most 0.0012.
Values may be sent and summed in bfloat16 or wider, within the bound.
A program may use at most 64 MiB of HBM per device.

v0:
```python
import jax
import jax.numpy as jnp
from jax import lax
from jax.sharding import PartitionSpec as P


def pair_tile(query_emb, key_emb):
    return lax.dot_general(
        query_emb, key_emb, (((1,), (1,)), ((), ())), preferred_element_type=jnp.float32
    )


def on_device(states, projection, owner_group, cluster_sub, priority):
    num_dp = lax.axis_size("dp")
    doc_rows = states.shape[0]
    emb_width = projection.shape[1]
    slot_count = max(2, (2 * doc_rows + num_dp - 1) // num_dp)
    recv_rows = num_dp * slot_count
    projected = jnp.dot(states, projection, preferred_element_type=jnp.float32)
    square_sum = jnp.sum(projected * projected, axis=1, keepdims=True)
    inverse_norm = lax.rsqrt(square_sum + 1e-06)
    embedding = (projected * inverse_norm).astype(jnp.bfloat16)
    owner_row = owner_group[:, 0]
    onehot = (owner_row[:, None] == jnp.arange(num_dp, dtype=jnp.int32)[None, :]).astype(jnp.int32)
    slot_place = jnp.sum(onehot * (jnp.cumsum(onehot, axis=0) - 1), axis=1)
    target = owner_row * slot_count + slot_place
    send_emb = jnp.zeros((recv_rows, emb_width), jnp.bfloat16).at[target].set(embedding)
    send_sub = jnp.full((recv_rows,), -1, jnp.int32).at[target].set(cluster_sub)
    send_prio = jnp.zeros((recv_rows,), jnp.int32).at[target].set(priority)
    got_emb, got_sub, got_prio = (
        lax.all_to_all(
            send_emb.reshape(num_dp, slot_count, emb_width),
            "dp",
            split_axis=0,
            concat_axis=0,
            tiled=True,
        ),
        lax.all_to_all(
            send_sub.reshape(num_dp, slot_count), "dp", split_axis=0, concat_axis=0, tiled=True
        ),
        lax.all_to_all(
            send_prio.reshape(num_dp, slot_count), "dp", split_axis=0, concat_axis=0, tiled=True
        ),
    )
    member_emb = got_emb.reshape(recv_rows, emb_width)
    member_sub = got_sub.reshape(recv_rows)
    member_prio = got_prio.reshape(recv_rows)
    lowest = jnp.full((recv_rows,), -1.0, jnp.float32)
    cosine = pair_tile(member_emb, lax.all_gather(member_emb, "grp", axis=0, tiled=True))
    earlier = (
        member_sub[:, None] == lax.all_gather(member_sub, "grp", axis=0, tiled=True)[None, :]
    ) & (lax.all_gather(member_prio, "grp", axis=0, tiled=True)[None, :] < member_prio[:, None])
    running = jnp.maximum(lowest, jnp.max(jnp.where(earlier, cosine, -1.0), axis=1))
    result_back = lax.all_to_all(
        running.reshape(num_dp, slot_count), "dp", split_axis=0, concat_axis=0, tiled=True
    )
    return result_back.reshape(recv_rows)[target]


def solution(mesh):
    in_specs = (
        P(("dp", "grp"), None),
        P(),
        P(("dp", "grp"), None),
        P(("dp", "grp")),
        P(("dp", "grp")),
    )
    out_specs = P(("dp", "grp"))
    return jax.shard_map(
        on_device, mesh=mesh, in_specs=in_specs, out_specs=out_specs, check_vma=False
    )
```

profile of v0, /device:TPU:1, one launch (start us, length us, event | category | flops | bytes accessed | tf_op | source)
XLA Modules:
  0.0 138.6 jit_solution(18221700818211266229)
XLA Ops:
  6.5 0.9 fusion.4
  7.4 0.2 reduce_window_sum.11
  7.6 0.8 select_reduce_fusion
  8.4 0.7 fusion.5
  9.1 1.7 %multiply_reduce_fusion = (f32[128]{0:T(128)S(1)}, f32[128,768]{1,0:T(8,128)S(1)}) fusion(bf16[128,2048]{1,0:T(8,128)(2,1)} %param.5, bf16[2048,768]{1,0:T(8,128)(2,1)S(1)} %copy-done), kind=kOutput, calls=%fused_computation.7 | convolution fusion | flops 402849664 | bytes 4063744 | tf_op jit(solution)/shard_map/dot_general | solution.py:19
  10.8 1.9 %scatter_custom_fusion.2 = bf16[256,768]{1,0:T(8,128)(2,1)} fusion(s32[128]{0:T(128)S(1)} %fusion.5, f32[128,768]{1,0:T(8,128)S(1)} %get-tuple-element.6, f32[128]{0:T(128)S(1)} %add_rsqrt_fusion, bf16[]{:T(256)} %constant.13.clone.1), kind=kCustom, calls=%fused_computation.8 | custom fusion | flops 196608 | bytes 786946 | tf_op jit(solution)/shard_map/scatter | solution.py:27
  12.7 1.1 reshape.54
  13.9 35.1 %all_to_all.29 = bf16[128,2,768]{2,1,0:T(2,128)(2,1)} all-to-all(bf16[128,2,768]{2,1,0:T(2,128)(2,1)S(1)} %reshape.54), channel_id=1, replica_groups=mesh['dp'=128,'grp'=4] {'dp'}, dimensions={0} | all-to-all | bytes 786432 | tf_op jit(solution)/shard_map/all_to_all | solution.py:31
  49.0 1.9 %reshape.55 = bf16[256,768]{1,0:T(8,128)(2,1)} reshape(bf16[128,2,768]{2,1,0:T(2,128)(2,1)} %all_to_all.29) | data formatting | bytes 786432 | tf_op jit(solution)/shard_map/reshape | solution.py:45
  50.9 1.1 scatter_custom_fusion
  52.0 0.8 all_to_all.19
  52.8 7.1 %all-to-all-start = ((s32[128,1,2]{2,1,0:T(1,128)}), s32[128,1,2]{2,1,0:T(1,128)S(1)}, u32[]{:S(2)}, u32[]{:S(2)}) async-start(s32[128,1,2]{2,1,0:T(1,128)} %bitcast.3), calls=%async_computation | async-start | bytes 131072 | tf_op jit(solution)/shard_map/all_to_all | solution.py:38
  59.9 1.1 scatter_custom_fusion.1
  61.0 0.8 all_to_all.21
  61.8 9.8 %all-to-all-done = s32[128,1,2]{2,1,0:T(1,128)S(1)} async-done(((s32[128,1,2]{2,1,0:T(1,128)}), s32[128,1,2]{2,1,0:T(1,128)S(1)}, u32[]{:S(2)}, u32[]{:S(2)}) %all-to-all-start) | async-done | bytes 1056 | tf_op jit(solution)/shard_map/all_to_all | solution.py:38
  71.6 5.7 %all-to-all-start.1 = ((s32[128,1,2]{2,1,0:T(1,128)}), s32[128,1,2]{2,1,0:T(1,128)S(1)}, u32[]{:S(2)}, u32[]{:S(2)}) async-start(s32[128,1,2]{2,1,0:T(1,128)} %bitcast.5), calls=%async_computation.1 | async-start | bytes 131072 | tf_op jit(solution)/shard_map/all_to_all | solution.py:41
  77.2 0.1 reshape.89
  77.4 11.5 %all-to-all-done.1 = s32[128,1,2]{2,1,0:T(1,128)S(1)} async-done(((s32[128,1,2]{2,1,0:T(1,128)}), s32[128,1,2]{2,1,0:T(1,128)S(1)}, u32[]{:S(2)}, u32[]{:S(2)}) %all-to-all-start.1) | async-done | bytes 1056 | tf_op jit(solution)/shard_map/all_to_all | solution.py:41
  89.0 0.5 broadcast.57
  89.5 0.8 reduce.13
  90.3 0.1 reshape.91
  90.5 0.8 reduce.14
  91.3 0.1 eq.34
  91.4 7.7 %all-gather = s32[4,1,256]{2,1,0:T(1,128)S(1)} all-gather(s32[1,1,256]{2,1,0:T(1,128)S(1)} %reshape.89), channel_id=1, replica_groups=mesh['dp'=128,'grp'=4] {'grp'}, dimensions={0}, use_global_device_ids=true | all-gather | bytes 5120 | tf_op jit(solution)/shard_map/all_gather | solution.py:51
  99.1 5.2 %all-gather.1 = s32[4,1,256]{2,1,0:T(1,128)S(1)} all-gather(s32[1,1,256]{2,1,0:T(1,128)S(1)} %reshape.91), channel_id=1, replica_groups=mesh['dp'=128,'grp'=4] {'grp'}, dimensions={0}, use_global_device_ids=true | all-gather | bytes 5120 | tf_op jit(solution)/shard_map/all_gather | solution.py:52
  104.3 2.3 %fusion = f32[256]{0:T(256)S(1)} fusion(bf16[256,768]{1,0:T(8,128)(2,1)} %reshape.55, bf16[1024,768]{1,0:T(8,128)(2,1)} %all-gather.4.cloned.1.call-done, s32[1024]{0:T(1024)S(1)} %bitcast.24, s32[1024]{0:T(1024)S(1)} %bitcast.23, s32[256]{0:T(256)S(1)} %reshape.53, s32[256]{0:T(256)S(1)} %eq.34), kind=kOutput, calls=%fused_computation.5 | convolution fusion | flops 403963648 | bytes 1977344 | tf_op jit(solution)/shard_map/dot_general | solution.py:8
  106.6 0.8 max_broadcast_in_dim.15
  107.4 9.5 %all-to-all-start.3 = ((f32[128,1,2]{2,1,0:T(1,128)}), f32[128,1,2]{2,1,0:T(1,128)S(1)}, u32[]{:S(2)}, u32[]{:S(2)}) async-start(f32[128,1,2]{2,1,0:T(1,128)} %bitcast.7), calls=%async_computation.3 | async-start | bytes 131072 | tf_op jit(solution)/shard_map/all_to_all | solution.py:54
  116.9 11.6 %all-to-all-done.3 = f32[128,1,2]{2,1,0:T(1,128)S(1)} async-done(((f32[128,1,2]{2,1,0:T(1,128)}), f32[128,1,2]{2,1,0:T(1,128)S(1)}, u32[]{:S(2)}, u32[]{:S(2)}) %all-to-all-start.3) | async-done | bytes 1056 | tf_op jit(solution)/shard_map/all_to_all | solution.py:54
  128.5 0.5 broadcast.59
  129.0 0.8 reduce.15
  130.0 1.8 %gather_fusion = f32[128]{0:T(128)} fusion(f32[256]{0:T(256)S(1)} %reshape.56, s32[1024]{0:T(1024)S(1)} %pad_clamp_fusion), kind=kCustom, calls=%fused_computation | custom fusion | bytes 1536 | tf_op jit(solution)/shard_map/gather | solution.py:57
  (10 shorter events, 0.3 us)
Async XLA Ops:
  6.5 2.6 %copy-start = (bf16[2048,768]{1,0:T(8,128)(2,1)S(1)}, bf16[2048,768]{1,0:T(8,128)(2,1)}, u32[]{:S(2)}) copy-start(bf16[2048,768]{1,0:T(8,128)(2,1)} %param.6) | copy-start | bytes 9437188
  6.5 97.8 %all-gather.4.cloned.1.call-start = ((), (), s32[]{:S(2)}) async-start(), calls=%async_computation.4 | async-start | bytes 1966080 | tf_op jit(solution)/shard_map/all_gather | solution.py:49
  52.8 18.8 %all-to-all-start = ((s32[128,1,2]{2,1,0:T(1,128)}), s32[128,1,2]{2,1,0:T(1,128)S(1)}, u32[]{:S(2)}, u32[]{:S(2)}) async-start(s32[128,1,2]{2,1,0:T(1,128)} %bitcast.3), calls=%async_computation | async-start | bytes 131072 | tf_op jit(solution)/shard_map/all_to_all | solution.py:38
  71.6 17.3 %all-to-all-start.1 = ((s32[128,1,2]{2,1,0:T(1,128)}), s32[128,1,2]{2,1,0:T(1,128)S(1)}, u32[]{:S(2)}, u32[]{:S(2)}) async-start(s32[128,1,2]{2,1,0:T(1,128)} %bitcast.5), calls=%async_computation.1 | async-start | bytes 131072 | tf_op jit(solution)/shard_map/all_to_all | solution.py:41
  107.4 21.1 %all-to-all-start.3 = ((f32[128,1,2]{2,1,0:T(1,128)}), f32[128,1,2]{2,1,0:T(1,128)S(1)}, u32[]{:S(2)}, u32[]{:S(2)}) async-start(f32[128,1,2]{2,1,0:T(1,128)} %bitcast.7), calls=%async_computation.3 | async-start | bytes 131072 | tf_op jit(solution)/shard_map/all_to_all | solution.py:54
Sparse Core Ops, SparseCore 0:
  51.0 25.2 all-gather.3
where the time goes:
time: 139 us
  blocking collectives  48.1 us (35%)
  waiting for transfers between devices  32.9 us (24%)
  starting transfers between devices  22.3 us (16%)
  between operations  13.5 us (10%)
  local copies, waits for them, and re-layouts  11 us (8%)
  other arithmetic  6.92 us (5%)
  matrix products  3.96 us (3%)
    all_to_all x1, blocking collectives, on_device(): lax.all_to_all(send_emb.reshape(num_dp, slot_count, emb_width), 'dp', spl...  35.1 us
    all_to_all x1, waiting for transfers between devices, on_device(): lax.all_to_all(running.reshape(num_dp, slot_count), 'dp', split_axis=0, c...  11.6 us
    all_to_all x1, waiting for transfers between devices, on_device(): lax.all_to_all(send_prio.reshape(num_dp, slot_count), 'dp', split_axis=0,...  11.5 us
    all_to_all x1, waiting for transfers between devices, on_device(): lax.all_to_all(send_sub.reshape(num_dp, slot_count), 'dp', split_axis=0,...  9.76 us
    all_to_all x1, starting transfers between devices, on_device(): lax.all_to_all(running.reshape(num_dp, slot_count), 'dp', split_axis=0, c...  9.48 us
    all_gather x1, blocking collectives, on_device(): lax.all_gather(member_sub, 'grp', axis=0, tiled=True)[None, :]  7.7 us
    all_to_all x1, starting transfers between devices, on_device(): lax.all_to_all(send_sub.reshape(num_dp, slot_count), 'dp', split_axis=0,...  7.12 us
    all_to_all x1, starting transfers between devices, on_device(): lax.all_to_all(send_prio.reshape(num_dp, slot_count), 'dp', split_axis=0,...  5.65 us
  transfers between devices with their start and end apart: 4, of which 3 were waited for; matrix products, arithmetic and copies ran while one was open for 4% of the time, Pallas kernels for 0%

commit v1 on v0

v1 whole, which is shorter than its diff:
```python
import functools

import jax
import jax.numpy as jnp
from jax import lax
from jax.experimental import pallas as pl
from jax.experimental.pallas import tpu as pltpu
from jax.sharding import PartitionSpec as P

MESH = pl.DeviceIdType.MESH
NY = 8
NZ = 16
NG = 4
SLOTS = 2
NT = (((1,), (1,)), ((), ()))


def mm(a, b):
    return jnp.dot(a, b, preferred_element_type=jnp.float32)


def mm_nt(a, b):
    return lax.dot_general(a, b, NT, preferred_element_type=jnp.float32)


def iota(shape, axis):
    return lax.broadcasted_iota(jnp.int32, shape, axis)


def ones_where(cond):
    return jnp.where(cond, 1.0, 0.0).astype(jnp.bfloat16)


def kernel(
    st, pr, ow, su, pi, out,
    s1a, s1b, r1a, r1b, s2a, s2b, r2a, r2b,
    krow, xa, xb, xk, sc, sr, rb, tb, rr,
    y1s, y1r, z1s, z1r, z2s, z2r, y2s, y2r, xs, xr, b1s, b1r, b2s, b2r,
):
    docs = st.shape[0]
    width = pr.shape[1]
    half = width // 2
    rows = NY * NZ * SLOTS
    ygrp = NZ * SLOTS
    zgrp = NY * SLOTS
    dp = lax.axis_index("dp")
    grp = lax.axis_index("grp")
    my_y = dp // NZ
    my_z = dp % NZ

    def y_at(i):
        return (my_y + i) % NY

    def z_at(j):
        return (my_z + j) % NZ

    def g_at(i):
        return (grp + i) % NG

    def y_dev(i):
        return {"dp": y_at(i) * NZ + my_z}

    def z_dev(j):
        return {"dp": my_y * NZ + z_at(j)}

    def g_dev(i):
        return {"grp": g_at(i)}

    def copy(src, dst, ssem, rsem, i, dev):
        return pltpu.make_async_remote_copy(
            src_ref=src, dst_ref=dst, send_sem=ssem.at[i], recv_sem=rsem.at[i],
            device_id=dev, device_id_type=MESH,
        )

    def yrows(y):
        return pl.ds(pl.multiple_of(y * ygrp, ygrp), ygrp)

    def zrows(z):
        return pl.ds(pl.multiple_of(z * zgrp, zgrp), zgrp)

    barrier = pltpu.get_barrier_semaphore()
    for i in range(1, NY):
        pl.semaphore_signal(barrier, inc=1, device_id=y_dev(i), device_id_type=MESH)
    for j in range(1, NZ):
        pl.semaphore_signal(barrier, inc=1, device_id=z_dev(j), device_id_type=MESH)
    for i in range(1, NG):
        pl.semaphore_signal(barrier, inc=1, device_id=g_dev(i), device_id_type=MESH)

    projected = mm(st[...], pr[...])
    square_sum = jnp.sum(projected * projected, axis=1, keepdims=True)
    emb = (projected * lax.rsqrt(square_sum + 1e-06)).astype(jnp.bfloat16)

    owner = ow[...]
    onehot = iota((NY * NZ, docs), 0) == owner
    before = ones_where(iota((docs, docs), 0) < iota((docs, docs), 1))
    counts = mm(ones_where(onehot), before)
    place = jnp.sum(jnp.where(onehot, counts, 0.0), axis=0, keepdims=True).astype(jnp.int32)
    target = owner * SLOTS + place
    target_b = (owner % NZ) * zgrp + (owner // NZ) * SLOTS + place
    slot_row = iota((rows, docs), 0)
    pick_a = ones_where(slot_row == target)
    pick_b = ones_where(slot_row == target_b)
    prio = pi[...]
    line = iota((docs, docs), 0)
    meta = jnp.where(
        line == 0, su[...] + 1, jnp.where(line == 1, prio // 256, jnp.where(line == 2, prio % 256, 0))
    ).astype(jnp.float32).astype(jnp.bfloat16)
    s1a[:, :half] = mm(pick_a, emb[:, :half]).astype(jnp.bfloat16)
    s1a[:, half:] = mm_nt(pick_a, meta).astype(jnp.bfloat16)
    s1b[...] = mm(pick_b, emb[:, half:]).astype(jnp.bfloat16)

    r_i, c_i = iota((rows, rows), 0), iota((rows, rows), 1)
    to_z = ones_where(c_i == ((r_i // SLOTS) % NY) * ygrp + (r_i // zgrp) * SLOTS + r_i % SLOTS)
    to_y = ones_where(c_i == ((r_i // SLOTS) % NZ) * zgrp + (r_i // ygrp) * SLOTS + r_i % SLOTS)

    pl.semaphore_wait(barrier, NY + NZ + NG - 3)
    sent = []
    y1, z1 = [], []
    for i in range(1, NY):
        c = copy(s1a.at[yrows(y_at(i)), :], r1a.at[yrows(my_y), :], y1s, y1r, i, y_dev(i))
        c.start()
        y1.append(c)
    for j in range(1, NZ):
        c = copy(s1b.at[zrows(z_at(j)), :], r1b.at[zrows(my_z), :], z1s, z1r, j, z_dev(j))
        c.start()
        z1.append(c)
    r1a[yrows(my_y), :] = s1a[yrows(my_y), :]
    r1b[zrows(my_z), :] = s1b[zrows(my_z), :]
    for c in y1:
        c.wait_recv()
    s2a[...] = mm(to_z, r1a[...]).astype(jnp.bfloat16)
    z2, y2 = [], []
    for j in range(1, NZ):
        c = copy(s2a.at[zrows(z_at(j)), :], r2a.at[zrows(my_z), :], z2s, z2r, j, z_dev(j))
        c.start()
        z2.append(c)
    r2a[zrows(my_z), :] = s2a[zrows(my_z), :]
    for c in z1:
        c.wait_recv()
    s2b[...] = mm(to_y, r1b[...]).astype(jnp.bfloat16)
    for i in range(1, NY):
        c = copy(s2b.at[yrows(y_at(i)), :], r2b.at[yrows(my_y), :], y2s, y2r, i, y_dev(i))
        c.start()
        y2.append(c)
    r2b[yrows(my_y), :] = s2b[yrows(my_y), :]

    for c in z2:
        c.wait_recv()
    qa = r2a[:, :half]
    qmeta = r2a[:, half:]
    w_row = iota((128, 128), 0)
    w_col = iota((128, 128), 1)

    def weights(at):
        return jnp.where(
            at == 0, 65536.0, jnp.where(at == 1, 256.0, jnp.where(at == 2, 1.0, 0.0))
        ).astype(jnp.bfloat16)

    krow[...] = mm_nt(weights(w_col)[:16], qmeta)[:8] - 65536.0
    ax1 = copy(r2a.at[:, pl.ds(0, half)], xa.at[0], xs, xr, 0, g_dev(1))
    ax2 = copy(r2a.at[:, pl.ds(0, half)], xa.at[1], xs, xr, 1, g_dev(NG - 1))
    ax1.start()
    ax2.start()
    kx = []
    for i in range(1, NG):
        c = copy(krow, xk.at[i - 1], xs, xr, 5 + i, g_dev(i))
        c.start()
        kx.append(c)
    for c in y2:
        c.wait_recv()
    bx2 = copy(r2b, xb.at[1], xs, xr, 3, g_dev(NG - 1))
    bx1 = copy(r2b, xb.at[0], xs, xr, 2, g_dev(1))
    bx2.start()
    bx1.start()

    qval = mm(qmeta, weights(w_row)) - 65536.0
    qbase = mm(qmeta, jnp.where(w_row == 0, 65536.0, 0.0).astype(jnp.bfloat16)) - 65536.0
    qb = mm(to_z, r2b[...]).astype(jnp.bfloat16)

    def fold(acc, ka, kb, keys):
        cosine = mm_nt(qa, ka) + mm_nt(qb, kb)
        for lane in range(0, rows, 128):
            key = keys[0:1, lane : lane + 128]
            ok = (key >= qbase) & (key < qval)
            acc = jnp.maximum(acc, jnp.where(ok, cosine[:, lane : lane + 128], -1.0))
        return acc

    acc = fold(jnp.full((rows, 128), -1.0, jnp.float32), qa, qb, krow[...])
    ax1.wait_recv()
    af = copy(xa.at[0], xa.at[2], xs, xr, 4, g_dev(1))
    af.start()
    bx2.wait_recv()
    bf = copy(xb.at[1], xb.at[2], xs, xr, 5, g_dev(NG - 1))
    bf.start()
    for c in kx:
        c.wait_recv()
    bx1.wait_recv()
    acc = fold(acc, xa[0], mm(to_z, xb[0]).astype(jnp.bfloat16), xk[0])
    ax2.wait_recv()
    acc = fold(acc, xa[1], mm(to_z, xb[1]).astype(jnp.bfloat16), xk[2])
    af.wait_recv()
    bf.wait_recv()
    acc = fold(acc, xa[2], mm(to_z, xb[2]).astype(jnp.bfloat16), xk[1])

    best = jnp.max(jnp.transpose(acc), axis=0, keepdims=True)
    per = 128 // zgrp
    for h in range(rows // 128):
        sc[h] = best[:, h * 128 : (h + 1) * 128]
    b1, b2 = [], []
    for j in range(1, NZ):
        c = copy(sc.at[z_at(j) // per], sr.at[my_z], b1s, b1r, j, z_dev(j))
        c.start()
        b1.append(c)
    sr[my_z] = sc[my_z // per]
    rb[...] = jnp.zeros_like(rb)
    for c in b1:
        c.wait_recv()
    for z in range(NZ):
        rb[z : z + 1, :] = sr[z]
    tb[...] = jnp.transpose(rb[...])

    def back_rows(y):
        return pl.ds(pl.multiple_of((my_z % per) * zgrp + (y // 4) * 8, 8), 8)

    for i in range(1, NY):
        c = copy(tb.at[back_rows(y_at(i)), :], rr.at[my_y], b2s, b2r, i, y_dev(i))
        c.start()
        b2.append(c)
    rr[my_y] = tb[back_rows(my_y), :]
    target_col = jnp.transpose(jnp.broadcast_to(target.astype(jnp.float32), (docs, docs)))
    lanes = iota((docs, 128), 1)
    res = jnp.full((docs, 128), -2.0, jnp.float32)
    for c in b2:
        c.wait_recv()
    for y in range(NY):
        for s in range(SLOTS):
            score = rr[y, pl.ds((my_y % 4) * SLOTS + s, 1), :]
            code = jnp.where(lanes < NZ, (y * NZ + lanes) * SLOTS + s, -1).astype(jnp.float32)
            res = jnp.where(target_col == code, score, res)
    out[...] = jnp.max(jnp.transpose(res), axis=0, keepdims=True)

    sent = y1 + z1 + z2 + y2 + [ax1, ax2, bx1, bx2, af, bf] + kx + b1 + b2
    for c in sent:
        c.wait_send()


def on_device(states, projection, owner_group, cluster_sub, priority):
    docs = states.shape[0]
    width = projection.shape[1]
    half = width // 2
    rows = NY * NZ * SLOTS
    bf, f32 = jnp.bfloat16, jnp.float32
    vmem = pl.BlockSpec(memory_space=pltpu.VMEM)
    dma = pltpu.SemaphoreType.DMA
    score = pl.pallas_call(
        kernel,
        out_shape=jax.ShapeDtypeStruct((1, docs), f32),
        in_specs=[vmem] * 5,
        out_specs=vmem,
        scratch_shapes=[
            pltpu.VMEM((rows, half + 128), bf),
            pltpu.VMEM((rows, half), bf),
            pltpu.VMEM((rows, half + 128), bf),
            pltpu.VMEM((rows, half), bf),
            pltpu.VMEM((rows, half + 128), bf),
            pltpu.VMEM((rows, half), bf),
            pltpu.VMEM((rows, half + 128), bf),
            pltpu.VMEM((rows, half), bf),
            pltpu.VMEM((8, rows), f32),
            pltpu.VMEM((3, rows, half), bf),
            pltpu.VMEM((3, rows, half), bf),
            pltpu.VMEM((3, 8, rows), f32),
            pltpu.VMEM((rows // 128, 1, 128), f32),
            pltpu.VMEM((NZ, 1, 128), f32),
            pltpu.VMEM((128, 128), f32),
            pltpu.VMEM((128, 128), f32),
            pltpu.VMEM((NY, 8, 128), f32),
            dma((NY,)), dma((NY,)), dma((NZ,)), dma((NZ,)),
            dma((NZ,)), dma((NZ,)), dma((NY,)), dma((NY,)),
            dma((9,)), dma((9,)),
            dma((NZ,)), dma((NZ,)), dma((NY,)), dma((NY,)),
        ],
        compiler_params=pltpu.CompilerParams(
            collective_id=0, has_side_effects=True, vmem_limit_bytes=48 * 1024 * 1024
        ),
    )(
        states,
        projection,
        owner_group.reshape(1, docs),
        cluster_sub.reshape(1, docs),
        priority.reshape(1, docs),
    )
    return score.reshape(docs)


def solution(mesh):
    in_specs = (
        P(("dp", "grp"), None),
        P(),
        P(("dp", "grp"), None),
        P(("dp", "grp")),
        P(("dp", "grp")),
    )
    return jax.shard_map(
        on_device, mesh=mesh, in_specs=in_specs, out_specs=P(("dp", "grp")), check_vma=False
    )
```

time: 139 us -> 64.5 us (0.46)
  Pallas kernels: 0 us -> 58.8 us
  blocking collectives: 48.1 us -> 0 us
  waiting for transfers between devices: 32.9 us -> 0 us
  starting transfers between devices: 22.3 us -> 0 us
  between operations: 13.5 us -> 0.01 us
  other arithmetic: 6.92 us -> 0 us
  local copies, waits for them, and re-layouts: 11 us -> 5.41 us
  matrix products: 3.96 us -> 0 us
    pallas_call x0 -> x1, Pallas kernels: none -> 58.8 us  [on_device(): pl.pallas_call(kernel, out_shape=jax.ShapeDtypeStruct((1, docs), f32), in...]
    all_to_all x1 -> x0, blocking collectives: 35.1 us -> none  [on_device(): lax.all_to_all(send_emb.reshape(num_dp, slot_count, emb_width), 'dp', spl...]
    all_to_all x3 -> x0, waiting for transfers between devices: 32.9 us -> none  [the longest x1 11.6 us: on_device(): lax.all_to_all(running.reshape(num_dp, slot_count), 'dp', split_axis=0, c...]
    all_to_all x3 -> x0, starting transfers between devices: 22.3 us -> none  [the longest x1 9.48 us: on_device(): lax.all_to_all(running.reshape(num_dp, slot_count), 'dp', split_axis=0, c...]
    all_gather x2 -> x0, blocking collectives: 12.9 us -> none  [the longest x1 7.7 us: on_device(): lax.all_gather(member_sub, 'grp', axis=0, tiled=True)[None, :]]
    unnamed x4 -> x11, local copies, waits for them, and re-layouts: 0.28 us -> 5.41 us
    dot_general x2 -> x0, matrix products: 3.96 us -> none  [the longest x1 2.26 us: pair_tile(): lax.dot_general(query_emb, key_emb, (((1,), (1,)), ((), ())), preferred_e...]
    reshape x4 -> x0, local copies, waits for them, and re-layouts: 3.3 us -> none  [the longest x1 1.88 us: on_device(): member_emb = got_emb.reshape(recv_rows, emb_width)]
  transfers between devices with their start and end apart: 4 -> 0, of which waited for: 3 -> 0; matrix products, arithmetic and copies ran while one was open for 4% -> 0% of each run, Pallas kernels for 0% -> 0%
where the time goes in v1:
time: 64.5 us; the launch traced here: 64.3 us
  Pallas kernels  58.8 us (91%)
  local copies, waits for them, and re-layouts  5.41 us (8%)
    pallas_call x1, Pallas kernels, on_device(): pl.pallas_call(kernel, out_shape=jax.ShapeDtypeStruct((1, docs), f32), in...  58.8 us
    unnamed x11, local copies, waits for them, and re-layouts  5.41 us

profile of v1, /device:TPU:1, one launch (start us, length us, event | category | flops | bytes accessed | tf_op | source)
XLA Modules:
  0.0 64.3 jit_solution(8346778152258409705)
XLA Ops:
  0.0 0.0 copy-start
  0.0 1.9 %copy-done = bf16[2048,768]{1,0:T(8,128)(2,1)S(1)} copy-done((bf16[2048,768]{1,0:T(8,128)(2,1)S(1)}, bf16[2048,768]{1,0:T(8,128)(2,1)}, u32[]{:S(2)}) %copy-start) | copy-done | bytes 3145752
  1.9 0.0 copy-start.1
  1.9 1.0 %copy-done.1 = bf16[128,2048]{1,0:T(8,128)(2,1)S(1)} copy-done((bf16[128,2048]{1,0:T(8,128)(2,1)S(1)}, bf16[128,2048]{1,0:T(8,128)(2,1)}, u32[]{:S(2)}) %copy-start.1) | copy-done | bytes 524312
  2.9 0.0 copy-start.2
  2.9 0.7 %copy-done.2 = s32[128,1]{0,1:T(1,128)S(1)} copy-done((s32[128,1]{0,1:T(1,128)S(1)}, s32[128,1]{0,1:T(1,128)}, u32[]{:S(2)}) %copy-start.2) | copy-done | bytes 536
  3.6 0.0 copy-start.3
  3.6 0.7 %copy-done.3 = s32[128]{0:T(128)S(1)} copy-done((s32[128]{0:T(128)S(1)}, s32[128]{0:T(128)}, u32[]{:S(2)}) %copy-start.3) | copy-done | bytes 536
  4.2 0.0 copy-start.4
  4.2 0.7 %copy-done.4 = s32[128]{0:T(128)S(1)} copy-done((s32[128]{0:T(128)S(1)}, s32[128]{0:T(128)}, u32[]{:S(2)}) %copy-start.4) | copy-done | bytes 536
  4.9 58.8 %shard_map.55 = f32[1,128]{1,0:T(1,128)S(1)} custom-call(bf16[128,2048]{1,0:T(8,128)(2,1)S(1)} %copy-done.1, bf16[2048,768]{1,0:T(8,128)(2,1)S(1)} %copy-done, s32[1,128]{1,0:T(1,128)S(1)} %bitcast.4, s32[1,128]{1,0:T(1,128)S(1)} %bitcast.5, s32[1,128]{1,0:T(1,128)S(1)} %bitcast.6), custom_call_target="tpu_custom_call" | custom-call | tf_op jit(solution)/shard_map/pallas_call | solution.py:255
  63.8 0.5 copy.7
Async XLA Ops:
  0.0 1.9 %copy-start = (bf16[2048,768]{1,0:T(8,128)(2,1)S(1)}, bf16[2048,768]{1,0:T(8,128)(2,1)}, u32[]{:S(2)}) copy-start(bf16[2048,768]{1,0:T(8,128)(2,1)} %pr.1) | copy-start | bytes 9437188
  1.9 1.0 %copy-start.1 = (bf16[128,2048]{1,0:T(8,128)(2,1)S(1)}, bf16[128,2048]{1,0:T(8,128)(2,1)}, u32[]{:S(2)}) copy-start(bf16[128,2048]{1,0:T(8,128)(2,1)} %st.1) | copy-start | bytes 1572868
  2.9 0.7 %copy-start.2 = (s32[128,1]{0,1:T(1,128)S(1)}, s32[128,1]{0,1:T(1,128)}, u32[]{:S(2)}) copy-start(s32[128,1]{0,1:T(1,128)} %param.7) | copy-start | bytes 1540
  3.6 0.7 %copy-start.3 = (s32[128]{0:T(128)S(1)}, s32[128]{0:T(128)}, u32[]{:S(2)}) copy-start(s32[128]{0:T(128)} %param.8) | copy-start | bytes 1540
  4.2 0.7 %copy-start.4 = (s32[128]{0:T(128)S(1)}, s32[128]{0:T(128)}, u32[]{:S(2)}) copy-start(s32[128]{0:T(128)} %param.9) | copy-start | bytes 1540

commit v2 on v1

v2 whole, which is shorter than its diff:
```python
import functools

import jax
import jax.numpy as jnp
from jax import lax
from jax.experimental import pallas as pl
from jax.experimental.pallas import tpu as pltpu
from jax.sharding import PartitionSpec as P

MESH = pl.DeviceIdType.MESH
NY = 8
NZ = 16
NG = 4
SLOTS = 2
LOADS = 4
PARTS = 2
FIRST = 1
NT = (((1,), (1,)), ((), ()))
Y_FAR = sorted(range(1, NY), key=lambda i: -min(i, NY - i))
Z_FAR = sorted(range(1, NZ), key=lambda j: -min(j, NZ - j))


def mm(a, b):
    return jnp.dot(a, b, preferred_element_type=jnp.float32)


def mm_nt(a, b):
    return lax.dot_general(a, b, NT, preferred_element_type=jnp.float32)


def iota(shape, axis):
    return lax.broadcasted_iota(jnp.int32, shape, axis)


def ones_where(cond):
    return jnp.where(cond, 1.0, 0.0).astype(jnp.bfloat16)


def kernel(
    st_hbm, pr_hbm, ow_hbm, su_hbm, pi_hbm, out,
    st, pr, ow, su, pi, load,
    s1a, s1b, r1a, r1b, s2a, s2b, r2a, r2b,
    krow, xa, xb, xk, sc, sr, rb, tb, rr,
    y1s, y1r, z1s, z1r, z2s, z2r, y2s, y2r, xs, xr, b1s, b1r, b2s, b2r,
):
    docs = st.shape[0]
    depth, width = pr.shape
    half = width // 2
    meta_w = s1a.shape[1] - half
    parts = PARTS
    first = FIRST * 128
    x_cols = [(0, first), (first, half - first)]
    a_cols = [(0, meta_w + first), (meta_w + first, half - first)]
    step = depth // LOADS
    rows = NY * NZ * SLOTS
    ygrp = NZ * SLOTS
    zgrp = NY * SLOTS
    dp = lax.axis_index("dp")
    grp = lax.axis_index("grp")
    my_y = dp // NZ
    my_z = dp % NZ

    def y_at(i):
        return (my_y + i) % NY

    def z_at(j):
        return (my_z + j) % NZ

    def g_at(i):
        return (grp + i) % NG

    def y_dev(i):
        return {"dp": y_at(i) * NZ + my_z}

    def z_dev(j):
        return {"dp": my_y * NZ + z_at(j)}

    def g_dev(i):
        return {"grp": g_at(i)}

    def copy(src, dst, ssem, rsem, i, dev):
        return pltpu.make_async_remote_copy(
            src_ref=src, dst_ref=dst, send_sem=ssem.at[i], recv_sem=rsem.at[i],
            device_id=dev, device_id_type=MESH,
        )

    def yrows(y):
        return pl.ds(pl.multiple_of(y * ygrp, ygrp), ygrp)

    def zrows(z):
        return pl.ds(pl.multiple_of(z * zgrp, zgrp), zgrp)

    barrier = pltpu.get_barrier_semaphore()
    for i in range(1, NY):
        pl.semaphore_signal(barrier, inc=1, device_id=y_dev(i), device_id_type=MESH)
    for j in range(1, NZ):
        pl.semaphore_signal(barrier, inc=1, device_id=z_dev(j), device_id_type=MESH)
    for i in range(1, NG):
        pl.semaphore_signal(barrier, inc=1, device_id=g_dev(i), device_id_type=MESH)

    loads = []
    for i, (src, dst) in enumerate(((ow_hbm, ow), (su_hbm, su), (pi_hbm, pi))):
        loads.append(pltpu.make_async_copy(src, dst, load.at[i]))
    for i in range(LOADS):
        cut = pl.ds(i * step, step)
        loads.append(pltpu.make_async_copy(st_hbm.at[:, cut], st.at[:, cut], load.at[3 + 2 * i]))
        loads.append(pltpu.make_async_copy(pr_hbm.at[cut, :], pr.at[cut, :], load.at[4 + 2 * i]))
    for c in loads:
        c.start()
    for c in loads[:3]:
        c.wait()
    owner = ow[...]
    onehot = iota((NY * NZ, docs), 0) == owner
    before = ones_where(iota((docs, docs), 0) < iota((docs, docs), 1))
    counts = mm(ones_where(onehot), before)
    place = jnp.sum(jnp.where(onehot, counts, 0.0), axis=0, keepdims=True).astype(jnp.int32)
    target = owner * SLOTS + place
    target_b = (owner % NZ) * zgrp + (owner // NZ) * SLOTS + place
    slot_row = iota((rows, docs), 0)
    pick_a = ones_where(slot_row == target)
    pick_b = ones_where(slot_row == target_b)
    prio = pi[...]
    line = iota((docs, docs), 0)
    meta = jnp.where(
        line == 0, su[...] + 1, jnp.where(line == 1, prio // 256, jnp.where(line == 2, prio % 256, 0))
    ).astype(jnp.float32).astype(jnp.bfloat16)
    r_i, c_i = iota((rows, rows), 0), iota((rows, rows), 1)
    y_bits, z_bits = NY.bit_length() - 1, NZ.bit_length() - 1
    slot, pair = r_i & 1, r_i >> 1
    to_z = ones_where(c_i == ((pair & (NY - 1)) * ygrp + (pair >> y_bits) * SLOTS + slot))
    to_y = ones_where(c_i == ((pair & (NZ - 1)) * zgrp + (pair >> z_bits) * SLOTS + slot))

    s1a[:, :meta_w] = mm_nt(pick_a, meta).astype(jnp.bfloat16)

    projected = jnp.zeros((docs, width), jnp.float32)
    for i in range(LOADS):
        loads[3 + 2 * i].wait()
        loads[4 + 2 * i].wait()
        projected += mm(st[:, i * step : (i + 1) * step], pr[i * step : (i + 1) * step, :])
    square_sum = jnp.sum(projected * projected, axis=1, keepdims=True)
    emb = (projected * lax.rsqrt(square_sum + 1e-06)).astype(jnp.bfloat16)

    sent = []

    def start(c):
        c.start()
        sent.append(c)
        return c

    def arrive(copies):
        for c in copies:
            c.wait_recv()

    def over_y(src, dst, cols, ssem, rsem):
        lanes = pl.ds(*cols)
        copies = [
            start(copy(src.at[yrows(y_at(i)), lanes], dst.at[yrows(my_y), lanes], ssem, rsem, i, y_dev(i)))
            for i in Y_FAR
        ]
        dst[yrows(my_y), lanes] = src[yrows(my_y), lanes]
        return copies

    def over_z(src, dst, cols, ssem, rsem):
        lanes = pl.ds(*cols)
        copies = [
            start(copy(src.at[zrows(z_at(j)), lanes], dst.at[zrows(my_z), lanes], ssem, rsem, j, z_dev(j)))
            for j in Z_FAR
        ]
        dst[zrows(my_z), lanes] = src[zrows(my_z), lanes]
        return copies

    def order(perm, src, dst, cols):
        lanes = pl.ds(*cols)
        dst[:, lanes] = mm(perm, src[:, lanes]).astype(jnp.bfloat16)

    a1, b1_, a2, b2_ = [], [], [], []
    for n in range(parts):
        at, size = x_cols[n]
        s1b[:, at : at + size] = mm(pick_b, emb[:, half + at : half + at + size]).astype(jnp.bfloat16)
        s1a[:, meta_w + at : meta_w + at + size] = mm(pick_a, emb[:, at : at + size]).astype(jnp.bfloat16)
        if n == 0:
            pl.semaphore_wait(barrier, NY + NZ + NG - 3)
        b1_.append(over_z(s1b, r1b, x_cols[n], z1s.at[n], z1r.at[n]))
        a1.append(over_y(s1a, r1a, a_cols[n], y1s.at[n], y1r.at[n]))
    for n in range(parts):
        arrive(b1_[n])
        order(to_y, r1b, s2b, x_cols[n])
        b2_.append(over_y(s2b, r2b, x_cols[n], y2s.at[n], y2r.at[n]))
        arrive(a1[n])
        order(to_z, r1a, s2a, a_cols[n])
        a2.append(over_z(s2a, r2a, a_cols[n], z2s.at[n], z2r.at[n]))

    up, down = g_dev(1), g_dev(NG - 1)

    def spread(src, dst, first, cols, base):
        to = pl.ds(*cols)
        frm = pl.ds(cols[0] + first, cols[1])
        c1 = start(copy(src.at[:, frm], dst.at[0, :, to], xs, xr, base, up))
        c2 = start(copy(src.at[:, frm], dst.at[1, :, to], xs, xr, base + 1, down))
        return c1, c2

    def onward(dst, held, cols, base, dev):
        to = pl.ds(*cols)
        return start(copy(dst.at[held, :, to], dst.at[2, :, to], xs, xr, base + 2, dev))

    w_row = iota((128, 128), 0)
    w_col = iota((128, 128), 1)

    def weights(at):
        return jnp.where(
            at == 0, 65536.0, jnp.where(at == 1, 256.0, jnp.where(at == 2, 1.0, 0.0))
        ).astype(jnp.bfloat16)

    xas, xbs, fas, fbs = [], [], [], []

    def forward_b(n):
        xbs[n][1].wait_recv()
        fbs.append(onward(xb, 1, x_cols[n], 6 * n, down))

    def forward_a(n):
        xas[n][0].wait_recv()
        fas.append(onward(xa, 0, x_cols[n], 6 * n + 3, up))

    for n in range(parts):
        arrive(b2_[n])
        xbs.append(spread(r2b, xb, 0, x_cols[n], 6 * n))
        if n:
            forward_b(n - 1)
        arrive(a2[n])
        xas.append(spread(r2a, xa, meta_w, x_cols[n], 6 * n + 3))
        if n:
            forward_a(n - 1)
        else:
            qmeta = r2a[:, :meta_w]
            krow[...] = mm_nt(weights(w_col)[:16], qmeta)[:8] - 65536.0
            kx = [
                start(copy(krow, xk.at[i - 1], xs, xr, 6 * parts + i - 1, g_dev(i)))
                for i in range(1, NG)
            ]
    forward_b(parts - 1)
    forward_a(parts - 1)
    qval = mm(qmeta, weights(w_row)) - 65536.0
    qbase = mm(qmeta, jnp.where(w_row == 0, 65536.0, 0.0).astype(jnp.bfloat16)) - 65536.0
    qa = r2a[:, meta_w:]
    qb = mm(to_z, r2b[...]).astype(jnp.bfloat16)

    def fold(acc, cosine, keys):
        for lane in range(0, rows, 128):
            key = keys[0:1, lane : lane + 128]
            ok = (key >= qbase) & (key < qval)
            acc = jnp.maximum(acc, jnp.where(ok, cosine[:, lane : lane + 128], -1.0))
        return acc

    def cosines(ka, kb):
        return mm_nt(qa, ka) + mm_nt(qb, mm(to_z, kb).astype(jnp.bfloat16))

    acc = fold(jnp.full((rows, 128), -1.0, jnp.float32), mm_nt(qa, qa) + mm_nt(qb, qb), krow[...])
    arrive(kx)
    arrive([c[0] for c in xbs])
    acc = fold(acc, cosines(xa[0], xb[0]), xk[0])
    arrive([c[1] for c in xas])
    acc = fold(acc, cosines(xa[1], xb[1]), xk[2])
    last = jnp.zeros((rows, rows), jnp.float32)
    for n in range(parts):
        cut = slice(x_cols[n][0], sum(x_cols[n]))
        fbs[n].wait_recv()
        last += mm_nt(qb[:, cut], mm(to_z, xb[2, :, cut]).astype(jnp.bfloat16))
        fas[n].wait_recv()
        last += mm_nt(qa[:, cut], xa[2, :, cut])
    acc = fold(acc, last, xk[1])

    best = jnp.max(jnp.transpose(acc), axis=0, keepdims=True)
    per = 128 // zgrp
    for h in range(rows // 128):
        sc[h] = best[:, h * 128 : (h + 1) * 128]
    b1, b2 = [], []
    for j in Z_FAR:
        c = copy(sc.at[z_at(j) // per], sr.at[my_z], b1s, b1r, j, z_dev(j))
        b1.append(start(c))
    sr[my_z] = sc[my_z // per]
    rb[...] = jnp.zeros_like(rb)
    for c in b1:
        c.wait_recv()
    for z in range(NZ):
        rb[z : z + 1, :] = sr[z]
    tb[...] = jnp.transpose(rb[...])

    def back_rows(y):
        return pl.ds(pl.multiple_of((my_z % per) * zgrp + (y // 4) * 8, 8), 8)

    for i in Y_FAR:
        c = copy(tb.at[back_rows(y_at(i)), :], rr.at[my_y], b2s, b2r, i, y_dev(i))
        b2.append(start(c))
    rr[my_y] = tb[back_rows(my_y), :]
    target_col = jnp.transpose(jnp.broadcast_to(target.astype(jnp.float32), (docs, docs)))
    lanes = iota((1, 128), 1)
    res = jnp.full((docs, 128), -2.0, jnp.float32)
    for c in sent[: -len(b2)]:
        c.wait_send()
    for c in b2:
        c.wait_recv()
    for y in range(NY):
        for s in range(SLOTS):
            score = rr[y, pl.ds((my_y % 4) * SLOTS + s, 1), :]
            code = jnp.where(lanes < NZ, (y * NZ + lanes) * SLOTS + s, -1).astype(jnp.float32)
            res = jnp.where(target_col == code, score, res)
    out[...] = jnp.max(jnp.transpose(res), axis=0, keepdims=True)

    for c in b2:
        c.wait_send()


def on_device(states, projection, owner_group, cluster_sub, priority):
    docs = states.shape[0]
    width = projection.shape[1]
    half = width // 2
    parts = PARTS
    rows = NY * NZ * SLOTS
    bf, f32 = jnp.bfloat16, jnp.float32
    vmem = pl.BlockSpec(memory_space=pltpu.VMEM)
    dma = pltpu.SemaphoreType.DMA
    score = pl.pallas_call(
        kernel,
        out_shape=jax.ShapeDtypeStruct((1, docs), f32),
        in_specs=[pl.BlockSpec(memory_space=pltpu.HBM)] * 5,
        out_specs=vmem,
        scratch_shapes=[
            pltpu.VMEM(states.shape, bf),
            pltpu.VMEM(projection.shape, bf),
            pltpu.VMEM((1, docs), jnp.int32),
            pltpu.VMEM((1, docs), jnp.int32),
            pltpu.VMEM((1, docs), jnp.int32),
            dma((3 + 2 * LOADS,)),
            pltpu.VMEM((rows, half + 128), bf),
            pltpu.VMEM((rows, half), bf),
            pltpu.VMEM((rows, half + 128), bf),
            pltpu.VMEM((rows, half), bf),
            pltpu.VMEM((rows, half + 128), bf),
            pltpu.VMEM((rows, half), bf),
            pltpu.VMEM((rows, half + 128), bf),
            pltpu.VMEM((rows, half), bf),
            pltpu.VMEM((8, rows), f32),
            pltpu.VMEM((3, rows, half), bf),
            pltpu.VMEM((3, rows, half), bf),
            pltpu.VMEM((3, 8, rows), f32),
            pltpu.VMEM((rows // 128, 1, 128), f32),
            pltpu.VMEM((NZ, 1, 128), f32),
            pltpu.VMEM((128, 128), f32),
            pltpu.VMEM((128, 128), f32),
            pltpu.VMEM((NY, 8, 128), f32),
            dma((parts, NY)), dma((parts, NY)), dma((parts, NZ)), dma((parts, NZ)),
            dma((parts, NZ)), dma((parts, NZ)), dma((parts, NY)), dma((parts, NY)),
            dma((6 * parts + NG - 1,)), dma((6 * parts + NG - 1,)),
            dma((NZ,)), dma((NZ,)), dma((NY,)), dma((NY,)),
        ],
        compiler_params=pltpu.CompilerParams(
            collective_id=0, has_side_effects=True, vmem_limit_bytes=67043328
        ),
    )(
        states,
        projection,
        owner_group.reshape(1, docs),
        cluster_sub.reshape(1, docs),
        priority.reshape(1, docs),
    )
    return score.reshape(docs)


def solution(mesh):
    in_specs = (
        P(("dp", "grp"), None),
        P(),
        P(("dp", "grp"), None),
        P(("dp", "grp")),
        P(("dp", "grp")),
    )
    return jax.shard_map(
        on_device, mesh=mesh, in_specs=in_specs, out_specs=P(("dp", "grp")), check_vma=False
    )
```

time: 64.5 us -> 55.4 us (0.86)
  Pallas kernels: 58.8 us -> 54.1 us
  local copies, waits for them, and re-layouts: 5.41 us -> 1.19 us
    pallas_call x1, Pallas kernels: 58.8 us -> 54.1 us  [on_device(): pl.pallas_call(kernel, out_shape=jax.ShapeDtypeStruct((1, docs), f32), in...]
    unnamed x11 -> x1, local copies, waits for them, and re-layouts: 5.41 us -> 1.19 us
where the time goes in v2:
time: 55.4 us; the launch traced here: 55.3 us
  Pallas kernels  54.1 us (98%)
  local copies, waits for them, and re-layouts  1.19 us (2%)
    pallas_call x1, Pallas kernels, on_device(): pl.pallas_call(kernel, out_shape=jax.ShapeDtypeStruct((1, docs), f32), in...  54.1 us
    unnamed x1, local copies, waits for them, and re-layouts  1.19 us

profile of v2, /device:TPU:1, one launch (start us, length us, event | category | flops | bytes accessed | tf_op | source)
XLA Modules:
  0.0 55.3 jit_solution(17488524741733756391)
XLA Ops:
  0.0 54.1 %shard_map.55 = f32[1,128]{1,0:T(1,128)} custom-call(bf16[128,2048]{1,0:T(8,128)(2,1)} %st_hbm.1, bf16[2048,768]{1,0:T(8,128)(2,1)} %pr_hbm.1, s32[1,128]{1,0:T(1,128)} %bitcast.4, s32[1,128]{1,0:T(1,128)} %bitcast.5, s32[1,128]{1,0:T(1,128)} %bitcast.6), custom_call_target="tpu_custom_call" | custom-call | tf_op jit(solution)/shard_map/pallas_call | solution.py:322
  54.1 1.2 %copy.7 = f32[128]{0:T(128)} copy(f32[128]{0:T(128)} %bitcast.7) | data formatting | bytes 1024

commit v3 on v2

--- a/solution.py
+++ b/solution.py
@@ -12,9 +12,10 @@
 NZ = 16
 NG = 4
 SLOTS = 2
-LOADS = 4
-PARTS = 2
-FIRST = 1
+LOADS = 2
+CUTS = (0, 1, 3)
+PARTS = len(CUTS) - 1
+LAG = 2
 NT = (((1,), (1,)), ((), ()))
 Y_FAR = sorted(range(1, NY), key=lambda i: -min(i, NY - i))
 Z_FAR = sorted(range(1, NZ), key=lambda j: -min(j, NZ - j))
@@ -48,9 +49,8 @@
     half = width // 2
     meta_w = s1a.shape[1] - half
     parts = PARTS
-    first = FIRST * 128
-    x_cols = [(0, first), (first, half - first)]
-    a_cols = [(0, meta_w + first), (meta_w + first, half - first)]
+    x_cols = [(lo * 128, (hi - lo) * 128) for lo, hi in zip(CUTS[:-1], CUTS[1:])]
+    a_cols = [(meta_w + at if at else 0, size if at else meta_w + size) for at, size in x_cols]
     step = depth // LOADS
     rows = NY * NZ * SLOTS
     ygrp = NZ * SLOTS
@@ -203,7 +203,6 @@
         to = pl.ds(*cols)
         return start(copy(dst.at[held, :, to], dst.at[2, :, to], xs, xr, base + 2, dev))
 
-    w_row = iota((128, 128), 0)
     w_col = iota((128, 128), 1)
 
     def weights(at):
@@ -224,55 +223,64 @@
     for n in range(parts):
         arrive(b2_[n])
         xbs.append(spread(r2b, xb, 0, x_cols[n], 6 * n))
-        if n:
-            forward_b(n - 1)
+        if n >= LAG:
+            forward_b(n - LAG)
         arrive(a2[n])
         xas.append(spread(r2a, xa, meta_w, x_cols[n], 6 * n + 3))
-        if n:
-            forward_a(n - 1)
-        else:
+        if n >= LAG:
+            forward_a(n - LAG)
+        if n == 0:
             qmeta = r2a[:, :meta_w]
             krow[...] = mm_nt(weights(w_col)[:16], qmeta)[:8] - 65536.0
             kx = [
                 start(copy(krow, xk.at[i - 1], xs, xr, 6 * parts + i - 1, g_dev(i)))
                 for i in range(1, NG)
             ]
-    forward_b(parts - 1)
-    forward_a(parts - 1)
-    qval = mm(qmeta, weights(w_row)) - 65536.0
-    qbase = mm(qmeta, jnp.where(w_row == 0, 65536.0, 0.0).astype(jnp.bfloat16)) - 65536.0
+            qval = krow[0:1, :]
+            whole = jnp.where(w_col == 0, 65536.0, 0.0).astype(jnp.bfloat16)
+            qbase = mm_nt(whole[:16], qmeta)[0:1] - 65536.0
+    for n in range(max(0, parts - LAG), parts):
+        forward_b(n)
+        forward_a(n)
     qa = r2a[:, meta_w:]
     qb = mm(to_z, r2b[...]).astype(jnp.bfloat16)
 
-    def fold(acc, cosine, keys):
-        for lane in range(0, rows, 128):
-            key = keys[0:1, lane : lane + 128]
-            ok = (key >= qbase) & (key < qval)
-            acc = jnp.maximum(acc, jnp.where(ok, cosine[:, lane : lane + 128], -1.0))
-        return acc
+    def column(keys):
+        tiles = [jnp.broadcast_to(keys[0:1, at : at + 128], (128, 128)) for at in range(0, rows, 128)]
+        return jnp.concatenate([jnp.transpose(t) for t in tiles], axis=0)
+
+    def fold(best, cosine, keys):
+        found = []
+        for h, old in enumerate(best):
+            cut = slice(h * 128, (h + 1) * 128)
+            ok = (keys >= qbase[:, cut]) & (keys < qval[:, cut])
+            top = jnp.max(jnp.where(ok, cosine[:, cut], -1.0), axis=0, keepdims=True)
+            found.append(jnp.maximum(old, top))
+        return found
 
     def cosines(ka, kb):
-        return mm_nt(qa, ka) + mm_nt(qb, mm(to_z, kb).astype(jnp.bfloat16))
-
-    acc = fold(jnp.full((rows, 128), -1.0, jnp.float32), mm_nt(qa, qa) + mm_nt(qb, qb), krow[...])
+        return mm_nt(ka, qa) + mm_nt(mm(to_z, kb).astype(jnp.bfloat16), qb)
+
+    best = [jnp.full((1, 128), -1.0, jnp.float32)] * (rows // 128)
+    best = fold(best, mm_nt(qa, qa) + mm_nt(qb, qb), column(krow[...]))
     arrive(kx)
+    keys = [column(xk[i]) for i in range(NG - 1)]
     arrive([c[0] for c in xbs])
-    acc = fold(acc, cosines(xa[0], xb[0]), xk[0])
+    best = fold(best, cosines(xa[0], xb[0]), keys[0])
     arrive([c[1] for c in xas])
-    acc = fold(acc, cosines(xa[1], xb[1]), xk[2])
+    best = fold(best, cosines(xa[1], xb[1]), keys[2])
     last = jnp.zeros((rows, rows), jnp.float32)
     for n in range(parts):
         cut = slice(x_cols[n][0], sum(x_cols[n]))
         fbs[n].wait_recv()
-        last += mm_nt(qb[:, cut], mm(to_z, xb[2, :, cut]).astype(jnp.bfloat16))
+        last += mm_nt(mm(to_z, xb[2, :, cut]).astype(jnp.bfloat16), qb[:, cut])
         fas[n].wait_recv()
-        last += mm_nt(qa[:, cut], xa[2, :, cut])
-    acc = fold(acc, last, xk[1])
-
-    best = jnp.max(jnp.transpose(acc), axis=0, keepdims=True)
+        last += mm_nt(xa[2, :, cut], qa[:, cut])
+    best = fold(best, last, keys[1])
+
     per = 128 // zgrp
     for h in range(rows // 128):
-        sc[h] = best[:, h * 128 : (h + 1) * 128]
+        sc[h] = best[h]
     b1, b2 = [], []
     for j in Z_FAR:
         c = copy(sc.at[z_at(j) // per], sr.at[my_z], b1s, b1r, j, z_dev(j))
@@ -354,14 +362,19 @@
             dma((NZ,)), dma((NZ,)), dma((NY,)), dma((NY,)),
         ],
         compiler_params=pltpu.CompilerParams(
-            collective_id=0, has_side_effects=True, vmem_limit_bytes=67043328
+            collective_id=0, has_side_effects=True, vmem_limit_bytes=48 * 1024 * 1024
         ),
     )(
-        states,
-        projection,
-        owner_group.reshape(1, docs),
-        cluster_sub.reshape(1, docs),
-        priority.reshape(1, docs),
+        *(
+            pltpu.with_memory_space_constraint(x, pltpu.HBM)
+            for x in (
+                states,
+                projection,
+                owner_group.reshape(1, docs),
+                cluster_sub.reshape(1, docs),
+                priority.reshape(1, docs),
+            )
+        ),
     )
     return score.reshape(docs)
 

time: 55.4 us -> 53.9 us (0.973)
  Pallas kernels: 54.1 us -> 53.3 us
  local copies, waits for them, and re-layouts: 1.19 us -> 0.51 us
    pallas_call x1, Pallas kernels: 54.1 us -> 53.3 us  [on_device(): pl.pallas_call(kernel, out_shape=jax.ShapeDtypeStruct((1, docs), f32), in...]
    unnamed x1, local copies, waits for them, and re-layouts: 1.19 us -> 0.51 us
where the time goes in v3:
time: 53.9 us; the launch traced here: 53.8 us
  Pallas kernels  53.3 us (99%)
    pallas_call x1, Pallas kernels, on_device(): pl.pallas_call(kernel, out_shape=jax.ShapeDtypeStruct((1, docs), f32), in...  53.3 us

profile of v3, /device:TPU:1, one launch (start us, length us, event | category | flops | bytes accessed | tf_op | source)
XLA Modules:
  0.0 53.8 jit_solution(10741957347206134203)
XLA Ops:
  0.0 53.3 %shard_map.55 = f32[1,128]{1,0:T(1,128)S(1)} custom-call(bf16[128,2048]{1,0:T(8,128)(2,1)} %st_hbm.1, bf16[2048,768]{1,0:T(8,128)(2,1)} %pr_hbm.1, s32[1,128]{1,0:T(1,128)} %bitcast.5, s32[1,128]{1,0:T(1,128)} %bitcast.6, s32[1,128]{1,0:T(1,128)} %bitcast.7), custom_call_target="tpu_custom_call" | custom-call | tf_op jit(solution)/shard_map/pallas_call | solution.py:330
  53.3 0.5 copy.7

commit v4 on v3

--- a/solution.py
+++ b/solution.py
@@ -180,8 +180,8 @@
         s1a[:, meta_w + at : meta_w + at + size] = mm(pick_a, emb[:, at : at + size]).astype(jnp.bfloat16)
         if n == 0:
             pl.semaphore_wait(barrier, NY + NZ + NG - 3)
+        a1.append(over_y(s1a, r1a, a_cols[n], y1s.at[n], y1r.at[n]))
         b1_.append(over_z(s1b, r1b, x_cols[n], z1s.at[n], z1r.at[n]))
-        a1.append(over_y(s1a, r1a, a_cols[n], y1s.at[n], y1r.at[n]))
     for n in range(parts):
         arrive(b1_[n])
         order(to_y, r1b, s2b, x_cols[n])

time: 53.9 us -> 54 us (level)
  no operation moved by 1% of the time
where the time goes in v4:
time: 54 us; the launch traced here: 53.8 us
  Pallas kernels  53.3 us (99%)
    pallas_call x1, Pallas kernels, on_device(): pl.pallas_call(kernel, out_shape=jax.ShapeDtypeStruct((1, docs), f32), in...  53.3 us

profile of v4, /device:TPU:1, one launch (start us, length us, event | category | flops | bytes accessed | tf_op | source)
XLA Modules:
  0.0 53.8 jit_solution(17989241112945354722)
XLA Ops:
  0.0 53.3 %shard_map.55 = f32[1,128]{1,0:T(1,128)S(1)} custom-call(bf16[128,2048]{1,0:T(8,128)(2,1)} %st_hbm.1, bf16[2048,768]{1,0:T(8,128)(2,1)} %pr_hbm.1, s32[1,128]{1,0:T(1,128)} %bitcast.5, s32[1,128]{1,0:T(1,128)} %bitcast.6, s32[1,128]{1,0:T(1,128)} %bitcast.7), custom_call_target="tpu_custom_call" | custom-call | tf_op jit(solution)/shard_map/pallas_call | solution.py:330
  53.3 0.5 copy.7
